TPU v7x, 32 devices: a whole 2x2x4 slice. The times are simulated.
32 devices in a mesh: ex: 8 (over y, x, core), co: 4 (over z).
Axes of the slice: x: 2, y: 2, z: 4, core: 2. Of those that a mesh axis runs over, the one named last changes fastest.
Arguments:
- train_grads: float32 [8192, 32768], P('ex', 'co')
- queries: float32 [1024, 32768], P('ex', 'co'), may hold values from -6 to 6
- module_ids: int32 [8], replicated, may hold values from 0 to 223
- module_scale: float32 [224], replicated, may hold values from 0.3 to 3
- example_ids: int32 [8192], P('ex'), may hold values from 0 to 8191, as said below
Outputs:
- influence: float32 [1024, 8192], P('co', 'ex')
Inputs may be any that keep to these rules, and one draw needn't show every extreme that they name: `example_ids`: the examples of block s of 1024 rows carry the ids s * 1024 to (s + 1) * 1024 - 1, each once.
All inputs are finite; a program needn't handle non-finite values.
Results may differ from a plain program's by a relative error of at most 0.00008.
Values sent between devices are 32-bit elements; how exact they have to be, the bound alone decides.
A program may use at most 128 MiB of HBM per device.

v0:
```python
import functools

import jax
import jax.numpy as jnp
from jax import lax
from jax.experimental import pallas as pl
from jax.experimental.pallas import tpu as pltpu
from jax.sharding import PartitionSpec as P

PROJ = 4096
MESH = pl.DeviceIdType.MESH
PIECES = 8
LEAD = 2
CONTRACT_LAST = (((1,), (1,)), ((), ()))

epsilon = 1e-06


def kernel(n_ex, n_co, pieces, q_ref, g_ref, scale_ref, out_ref, buf,
           ghi, glo, fresh, stage, split, part, got, sq_own, sq_got,
           ring_send, ring_recv, sib_send, sib_recv, part_send, part_recv, sq_send, sq_recv, load_sem):
    chips = n_ex // 2
    half = chips // 2
    ex = lax.axis_index("ex")
    co = lax.axis_index("co")
    core = ex % 2

    def snake(pos):
        upper = pos // half
        return pos * (1 - upper) + upper * (half + chips - 1 - pos)

    pos = snake(ex // 2)

    def device_at(step):
        return snake((pos + step + chips) % chips) * 2 + core

    right = device_at(1)
    left = device_at(-1)
    sibling = ex + 1 - 2 * core
    rows = q_ref.shape[0] // pieces
    width = q_ref.shape[1]
    mid = width // 2
    examples = g_ref.shape[0]
    owned = (n_ex // n_co) * rows

    barrier = pltpu.get_barrier_semaphore()
    for other in (right, left, sibling):
        pl.semaphore_signal(barrier, inc=1, device_id={"ex": other}, device_id_type=MESH)
    for k in range(1, n_co):
        pl.semaphore_signal(barrier, inc=1, device_id={"co": (co + k) % n_co}, device_id_type=MESH)
    pl.semaphore_wait(barrier, 3 + n_co - 1)

    def own_rows(s):
        return q_ref.at[pl.ds(pl.multiple_of(s * rows, rows), rows)]

    def ring_copy(way, d, s, arriving):
        back = d if arriving else d - 1
        origin = device_at(-back if way == 0 else back)
        if d == half and half > 1:
            span = pl.ds(way * mid, mid)
        else:
            span = pl.ds(0, width)
        if d == 1 and not arriving:
            src = own_rows(s)
        else:
            src = buf.at[s, origin, :, span]
        return pltpu.make_async_remote_copy(
            src_ref=src,
            dst_ref=buf.at[s, origin, :, span],
            send_sem=ring_send.at[way, d - 1, s],
            recv_sem=ring_recv.at[way, d - 1, s],
            device_id={"ex": right if way == 0 else left},
            device_id_type=MESH,
        )

    def sibling_copy(off, s, arriving):
        origin = device_at(off)
        if arriving:
            origin = origin + 1 - 2 * core
        src = own_rows(s) if off == 0 and not arriving else buf.at[s, origin]
        return pltpu.make_async_remote_copy(
            src_ref=src,
            dst_ref=buf.at[s, origin],
            send_sem=sib_send.at[off, s],
            recv_sem=sib_recv.at[off, s],
            device_id={"ex": sibling},
            device_id_type=MESH,
        )

    block = 256
    blocks = examples // block

    def part_copy(k, s, b):
        owner = (co + k) % n_co
        cols = pl.ds(pl.multiple_of(b * block, block), block)
        return pltpu.make_async_remote_copy(
            src_ref=part.at[s, pl.ds(pl.multiple_of(owner * owned, owned), owned), cols],
            dst_ref=got.at[k - 1, s, :, cols],
            send_sem=part_send.at[k - 1, s, b],
            recv_sem=part_recv.at[k - 1, s, b],
            device_id={"co": owner},
            device_id_type=MESH,
        )

    def sq_copy(k):
        return pltpu.make_async_remote_copy(
            src_ref=sq_own,
            dst_ref=sq_got.at[k - 1],
            send_sem=sq_send.at[k - 1],
            recv_sem=sq_recv.at[k - 1],
            device_id={"co": (co + k) % n_co},
            device_id_type=MESH,
        )

    def send_own(s):
        ring_copy(0, 1, s, False).start()
        ring_copy(1, 1, s, False).start()
        sibling_copy(0, s, False).start()

    for s in range(min(LEAD, pieces)):
        send_own(s)

    def relay(t):
        for d in range(1, half + 1):
            s = t - (d - 1)

            @pl.when((s >= 0) & (s < pieces))
            def _():
                ring_copy(0, d, s, True).wait_recv()
                if d < half:
                    ring_copy(0, d + 1, s, False).start()
                ring_copy(1, d, s, True).wait_recv()
                if d < half:
                    ring_copy(1, d + 1, s, False).start()
                if d == 1:
                    @pl.when(s + LEAD < pieces)
                    def _():
                        send_own(s + LEAD)
                sibling_copy(chips - d, s, False).start()
                if d < half:
                    sibling_copy(d, s, False).start()

    tile = fresh.shape[1]
    tiles = examples // tile
    strip = min(512, width)

    def g_load(i):
        slot = i % 2
        return pltpu.make_async_copy(
            g_ref.at[pl.ds(pl.multiple_of(i * tile, tile), tile)],
            fresh.at[slot],
            load_sem.at[slot],
        )

    g_load(0).start()

    def split_tile(i, sums):
        @pl.when(i + 1 < tiles)
        def _():
            g_load(i + 1).start()

        @pl.when(i == tiles // 2)
        def _():
            relay(0)

        g_load(i).wait()
        slot = i % 2
        dest = pl.multiple_of(i * tile, tile)

        def split_strip(j, total):
            col = pl.ds(pl.multiple_of(j * strip, strip), strip)
            x = fresh[slot, :, col]
            hi = x.astype(jnp.bfloat16)
            ghi[pl.ds(dest, tile), col] = hi
            glo[pl.ds(dest, tile), col] = (x - hi.astype(jnp.float32)).astype(jnp.bfloat16)
            xx = x * x
            for lane in range(0, strip, 128):
                total = total + xx[:, lane:lane + 128]
            return total

        total = lax.fori_loop(0, width // strip, split_strip, jnp.zeros((tile, 128), jnp.float32))
        row = jnp.sum(total.T, axis=0, keepdims=True)
        sq_own[:, pl.ds(dest, tile)] = jnp.broadcast_to(row, (8, tile))
        return sums

    lax.fori_loop(0, tiles, split_tile, 0)
    for k in range(1, n_co):
        sq_copy(k).start()

    depth = min(8192, width)
    count = n_ex * rows

    def load(off, side, s):
        origin = device_at(off)
        if side:
            origin = origin + 1 - 2 * core
        src = own_rows(s) if off == 0 and not side else buf.at[s, origin]
        return pltpu.make_async_copy(
            src,
            stage.at[pl.ds(pl.multiple_of(origin * rows, rows), rows)],
            load_sem.at[2 + off * 2 + side],
        )

    def compute(s):
        for off in range(chips):
            load(off, 0, s).start()
        for off in range(chips):
            sibling_copy(off, s, True).wait_recv()
            load(off, 1, s).start()
        for off in range(chips):
            load(off, 0, s).wait()
            load(off, 1, s).wait()

        def split_queries(j, c):
            col = pl.ds(pl.multiple_of(j * strip, strip), strip)
            x = stage[:, col] * scale_ref[:, col]
            hi = x.astype(jnp.bfloat16)
            split[pl.ds(0, count), col] = hi
            split[pl.ds(count, count), col] = (x - hi.astype(jnp.float32)).astype(jnp.bfloat16)
            return c

        lax.fori_loop(0, width // strip, split_queries, 0)

        def block_scores(b, c):
            ex_rows = pl.ds(pl.multiple_of(b * block, block), block)

            def deepen(j, acc):
                col = pl.ds(pl.multiple_of(j * depth, depth), depth)
                dot = functools.partial(
                    lax.dot_general, dimension_numbers=CONTRACT_LAST, preferred_element_type=jnp.float32
                )
                both = dot(split[:, col], ghi[ex_rows, col])
                small = both[count:] + dot(split[:count, col], glo[ex_rows, col])
                return acc + (small + both[:count])

            acc = lax.fori_loop(0, width // depth, deepen, jnp.zeros((count, block), jnp.float32))
            part[s, :, ex_rows] = acc
            for k in range(1, n_co):
                part_copy(k, s, b).start()
            return c

        lax.fori_loop(0, blocks, block_scores, 0)

    def step(t, c):
        @pl.when(t > 0)
        def _():
            relay(t)

        s = t - (half - 1)

        @pl.when((s >= 0) & (s < pieces))
        def _():
            compute(s)

        return c

    lax.fori_loop(0, pieces + half - 1, step, 0)

    for k in range(1, n_co):
        sq_copy(k).wait_recv()
    squares = sq_own[...]
    for k in range(1, n_co):
        squares = squares + sq_got[k - 1]
    inverse_norm = lax.rsqrt(squares[0:1] + epsilon)

    def finish(s, c):
        for k in range(1, n_co):
            for b in range(blocks):
                part_copy(k, s, b).wait_recv()
        total = part[s, pl.ds(pl.multiple_of(co * owned, owned), owned)]
        for k in range(1, n_co):
            total = total + got[k - 1, s]
        total = total * inverse_norm
        for i in range(n_ex // n_co):
            at = pl.multiple_of(i * rows * pieces + s * rows, rows)
            out_ref[pl.ds(at, rows), :] = total[i * rows:(i + 1) * rows]
        return c

    lax.fori_loop(0, pieces, finish, 0)

    def drain(s, c):
        for way in range(2):
            for d in range(1, half + 1):
                ring_copy(way, d, s, False).wait_send()
        for off in range(chips):
            sibling_copy(off, s, False).wait_send()
        for k in range(1, n_co):
            for b in range(blocks):
                part_copy(k, s, b).wait_send()
        return c

    lax.fori_loop(0, pieces, drain, 0)
    for k in range(1, n_co):
        sq_copy(k).wait_send()


def shards(n_ex, n_co, train_grads, queries, module_ids, module_scale, example_ids):
    examples, width = train_grads.shape
    position = lax.axis_index("co") * width + lax.iota(jnp.int32, width)
    table_index = lax.iota(jnp.int32, module_scale.shape[0])
    picked = jnp.sum(
        jnp.where(module_ids[:, None] == table_index[None, :], module_scale[None, :], 0.0), axis=1
    )
    window_index = lax.iota(jnp.int32, module_ids.shape[0])
    coord_scale = jnp.sum(
        jnp.where((position // PROJ)[:, None] == window_index[None, :], picked[None, :], 0.0), axis=1
    )

    chips = n_ex // 2
    pieces = min(PIECES, queries.shape[0] // 8)
    rows = queries.shape[0] // pieces
    count = n_ex * rows
    owned = (n_ex // n_co) * rows
    f32, bf16 = jnp.float32, jnp.bfloat16
    dma = pltpu.SemaphoreType.DMA
    normed, _ = pl.pallas_call(
        functools.partial(kernel, n_ex, n_co, pieces),
        out_shape=(
            jax.ShapeDtypeStruct((owned * pieces, examples), f32),
            jax.ShapeDtypeStruct((pieces, n_ex, rows, width), f32),
        ),
        in_specs=[
            pl.BlockSpec(memory_space=pl.ANY),
            pl.BlockSpec(memory_space=pl.ANY),
            pl.BlockSpec(memory_space=pltpu.VMEM),
        ],
        out_specs=(pl.BlockSpec(memory_space=pltpu.VMEM), pl.BlockSpec(memory_space=pl.ANY)),
        scratch_shapes=[
            pltpu.VMEM((examples, width), bf16),
            pltpu.VMEM((examples, width), bf16),
            pltpu.VMEM((2, min(128, examples), width), f32),
            pltpu.VMEM((count, width), f32),
            pltpu.VMEM((2 * count, width), bf16),
            pltpu.VMEM((pieces, count, examples), f32),
            pltpu.VMEM((n_co - 1, pieces, owned, examples), f32),
            pltpu.VMEM((8, examples), f32),
            pltpu.VMEM((n_co - 1, 8, examples), f32),
            dma((2, chips // 2, pieces)),
            dma((2, chips // 2, pieces)),
            dma((chips, pieces)),
            dma((chips, pieces)),
            dma((n_co - 1, pieces, examples // 256)),
            dma((n_co - 1, pieces, examples // 256)),
            dma((n_co - 1,)),
            dma((n_co - 1,)),
            dma((2 + n_ex,)),
        ],
        compiler_params=pltpu.CompilerParams(
            collective_id=0, has_side_effects=True, vmem_limit_bytes=67043328
        ),
    )(queries, train_grads, coord_scale[None, :])

    local_ids = example_ids - lax.axis_index("ex") * examples
    place = (local_ids[:, None] == lax.iota(jnp.int32, examples)[None, :]).astype(f32)
    return lax.dot_general(
        normed, place, (((1,), (0,)), ((), ())), precision=lax.Precision.HIGH, preferred_element_type=f32
    )


def solution(mesh):
    return jax.shard_map(
        functools.partial(shards, mesh.shape["ex"], mesh.shape["co"]),
        mesh=mesh,
        in_specs=(P("ex", "co"), P("ex", "co"), P(), P(), P("ex")),
        out_specs=P("co", "ex"),
        check_vma=False,
    )
```

profile of v0, /device:TPU:6, one launch (start us, length us, event | category | flops | bytes accessed | tf_op | source)
XLA Modules:
  0.0 177.6 jit_solution(3265582864541864781)
XLA Ops:
  0.0 0.9 select_reduce_fusion.1
  0.9 0.8 select_reduce_fusion
  1.7 171.4 %shard_map.55 = (f32[256,1024]{1,0:T(8,128)}, f32[8,8,16,8192]{3,2,1,0:T(8,128)}) custom-call(f32[128,8192]{1,0:T(8,128)} %q_ref.1, f32[1024,8192]{1,0:T(8,128)} %g_ref.1, f32[1,8192]{1,0:T(1,128)} %bitcast.2), custom_call_target="tpu_custom_call" | custom-call | tf_op jit(solution)/shard_map/pallas_call | solution.py:316
  173.0 0.7 broadcast_subtract_fusion
  173.7 3.9 %fusion = f32[256,1024]{1,0:T(8,128)} fusion(f32[256,1024]{1,0:T(8,128)} %get-tuple-element.6, s32[1024]{0:T(1024)S(1)} %broadcast_subtract_fusion), kind=kOutput, calls=%fused_computation.1 | convolution fusion | flops 1611661312 | bytes 2101248 | tf_op jit(solution)/shard_map/dot_general | solution.py:355
  (1 shorter events, 0.0 us)
where the time goes:
time: 181 us; the launch traced here: 178 us
  Pallas kernels  171 us (94%)
  matrix products  3.88 us (2%)
  other arithmetic  2.35 us (1%)
    pallas_call x1, Pallas kernels, shards(): pl.pallas_call(functools.partial(kernel, n_ex, n_co, pieces), out_shape=(...  171 us
    dot_general x1, matrix products, shards(): lax.dot_general(normed, place, (((1,), (0,)), ((), ())), precision=lax.Pr...  3.88 us

commit v1 on v0

--- a/solution.py
+++ b/solution.py
@@ -357,9 +357,477 @@
     )
 
 
+LEAD2 = 4
+
+
+def plane_kernel(n_ex, n_co, ids_ref, table_ref, q_ref, g_ref, cols_ref, out_ref, buf,
+                 ghi, glo, stage, split, part, got, tail_part, tail_got, place, sq_own, sq_got,
+                 own_send, own_recv, rel_send, rel_recv, sib_send, sib_recv,
+                 part_send, part_recv, tail_send, tail_recv, sq_send, sq_recv, load_sem, g_sem):
+    ex = lax.axis_index("ex")
+    co = lax.axis_index("co")
+    core = ex % 2
+    chip = ex // 2
+    cx = chip % 2
+    cy = chip // 2
+    rows = 8
+    pieces = q_ref.shape[0] // rows
+    width = q_ref.shape[1]
+    mid = width // 2
+    examples = g_ref.shape[0]
+    per_pass = 2 * rows
+    count = n_ex * per_pass
+    owned = 2 * per_pass
+    passes = pieces // 2
+    tail_rows = 2 * LEAD2 * rows
+
+    def chip_at(x):
+        fx = cx if x % 2 == 0 else 1 - cx
+        fy = cy if x < 2 else 1 - cy
+        return fy * 2 + fx
+
+    diag = chip_at(3)
+    sibling = ex + 1 - 2 * core
+    near = [chip_at(1) * 2 + core, chip_at(2) * 2 + core]
+
+    def origin(x, side):
+        return chip_at(x) * 2 + (core if side == 0 else 1 - core)
+
+    barrier = pltpu.get_barrier_semaphore()
+    for other in (near[0], near[1], sibling):
+        pl.semaphore_signal(barrier, inc=1, device_id={"ex": other}, device_id_type=MESH)
+    for k in range(1, n_co):
+        pl.semaphore_signal(barrier, inc=1, device_id={"co": (co + k) % n_co}, device_id_type=MESH)
+    pl.semaphore_wait(barrier, 3 + n_co - 1)
+
+    def own_rows(p):
+        return q_ref.at[pl.ds(pl.multiple_of(p * rows, rows), rows)]
+
+    def own_copy(way, p, arriving):
+        src = chip_at(way + 1) * 2 + core if arriving else ex
+        return pltpu.make_async_remote_copy(
+            src_ref=own_rows(p),
+            dst_ref=buf.at[p, src],
+            send_sem=own_send.at[way, p],
+            recv_sem=own_recv.at[way, p],
+            device_id={"ex": near[way]},
+            device_id_type=MESH,
+        )
+
+    def relay_copy(way, p, arriving):
+        src = origin(3, 0) if arriving else near[1 - way]
+        span = pl.ds(way * mid, mid)
+        return pltpu.make_async_remote_copy(
+            src_ref=buf.at[p, src, :, span],
+            dst_ref=buf.at[p, src, :, span],
+            send_sem=rel_send.at[way, p],
+            recv_sem=rel_recv.at[way, p],
+            device_id={"ex": near[way]},
+            device_id_type=MESH,
+        )
+
+    def sib_copy(x, p, arriving):
+        src = origin(x, 1 if arriving else 0)
+        return pltpu.make_async_remote_copy(
+            src_ref=own_rows(p) if x == 0 else buf.at[p, src],
+            dst_ref=buf.at[p, src],
+            send_sem=sib_send.at[x, p],
+            recv_sem=sib_recv.at[x, p],
+            device_id={"ex": sibling},
+            device_id_type=MESH,
+        )
+
+    block = 256
+    blocks = examples // block
+
+    def block_cols(b):
+        return pl.ds(pl.multiple_of(b * block, block), block)
+
+    def part_copy(k, u, b):
+        owner = (co + k) % n_co
+        return pltpu.make_async_remote_copy(
+            src_ref=part.at[u, pl.ds(pl.multiple_of(owner * owned, owned), owned), block_cols(b)],
+            dst_ref=got.at[k - 1, u, :, block_cols(b)],
+            send_sem=part_send.at[k - 1, u, b],
+            recv_sem=part_recv.at[k - 1, u, b],
+            device_id={"co": owner},
+            device_id_type=MESH,
+        )
+
+    above = (co > diag).astype(jnp.int32)
+    depth = co + above * (n_co - 1 - 2 * co)
+
+    def tail_copy(slot, b):
+        return pltpu.make_async_remote_copy(
+            src_ref=tail_part.at[:, block_cols(b)],
+            dst_ref=tail_got.at[slot, :, block_cols(b)],
+            send_sem=tail_send.at[b],
+            recv_sem=tail_recv.at[slot, b],
+            device_id={"co": (co + 1 - 2 * slot + n_co) % n_co},
+            device_id_type=MESH,
+        )
+
+    def sq_copy(k):
+        return pltpu.make_async_remote_copy(
+            src_ref=sq_own,
+            dst_ref=sq_got.at[k - 1],
+            send_sem=sq_send.at[k - 1],
+            recv_sem=sq_recv.at[k - 1],
+            device_id={"co": (co + k) % n_co},
+            device_id_type=MESH,
+        )
+
+    def send_own(p):
+        own_copy(0, p, False).start()
+        own_copy(1, p, False).start()
+        sib_copy(0, p, False).start()
+
+    for p in range(LEAD2):
+        send_own(p)
+
+    def forward(p):
+        own_copy(1, p, True).wait_recv()
+        relay_copy(0, p, False).start()
+        own_copy(0, p, True).wait_recv()
+        relay_copy(1, p, False).start()
+
+        @pl.when(p + LEAD2 < pieces)
+        def _():
+            send_own(p + LEAD2)
+
+        sib_copy(1, p, False).start()
+        sib_copy(2, p, False).start()
+
+    def share_diag(p):
+        relay_copy(0, p, True).wait_recv()
+        relay_copy(1, p, True).wait_recv()
+        sib_copy(3, p, False).start()
+
+    tile = stage.shape[1]
+    tiles = examples // tile
+    strip = min(512, width)
+
+    def g_load(i):
+        return pltpu.make_async_copy(
+            g_ref.at[pl.ds(pl.multiple_of(i * tile, tile), tile)], stage.at[i % 2], g_sem.at[i % 2]
+        )
+
+    g_load(0).start()
+
+    local = cols_ref[...] - ex * examples
+    for i in range(examples // 128):
+        spot = lax.broadcasted_iota(jnp.int32, (128, examples), 0) + i * 128
+        hot = (spot == local).astype(jnp.float32).astype(jnp.bfloat16)
+        place[:, i * 128:(i + 1) * 128] = hot.T
+
+    def split_tile(i, c):
+        @pl.when(i + 1 < tiles)
+        def _():
+            g_load(i + 1).start()
+
+        @pl.when(i == tiles - 2)
+        def _():
+            forward(0)
+
+        g_load(i).wait()
+        slot = i % 2
+        dest = pl.ds(pl.multiple_of(i * tile, tile), tile)
+
+        def split_strip(j, total):
+            col = pl.ds(pl.multiple_of(j * strip, strip), strip)
+            x = stage[slot, :, col]
+            hi = x.astype(jnp.bfloat16)
+            ghi[col, dest] = hi.T
+            glo[col, dest] = (x - hi.astype(jnp.float32)).astype(jnp.bfloat16).T
+            xx = x * x
+            for lane in range(0, strip, 128):
+                total = total + xx[:, lane:lane + 128]
+            return total
+
+        total = lax.fori_loop(0, width // strip, split_strip, jnp.zeros((tile, 128), jnp.float32))
+        row = jnp.sum(total.T, axis=0, keepdims=True)
+        sq_own[:, dest] = jnp.broadcast_to(row, (8, tile))
+        return c
+
+    lax.fori_loop(0, tiles, split_tile, 0)
+    for k in range(1, n_co):
+        sq_copy(k).start()
+
+    def load(x, side, p, slot, row, sem):
+        src = own_rows(p) if x == 0 and side == 0 else buf.at[p, origin(x, side)]
+        return pltpu.make_async_copy(src, stage.at[slot, pl.ds(pl.multiple_of(row, rows), rows)], sem)
+
+    def pass_load(x, side, j, u):
+        p = 2 * u + j - (LEAD2 if x == 3 else 0)
+        return load(x, side, p, u % 2, origin(x, side) * per_pass + j * rows, load_sem.at[x, side, j])
+
+    def split_queries(slot, m):
+        def body(j, c):
+            col = pl.ds(pl.multiple_of(j * strip, strip), strip)
+            scale = table_ref[ids_ref[(co * width + j * strip) // PROJ]]
+            x = stage[slot, :m, col] * scale
+            hi = x.astype(jnp.bfloat16)
+            split[pl.ds(0, m), col] = hi
+            split[pl.ds(m, m), col] = (x - hi.astype(jnp.float32)).astype(jnp.bfloat16)
+            return c
+
+        lax.fori_loop(0, width // strip, body, 0)
+
+    def scores(m, b):
+        cols = block_cols(b)
+        both = jnp.dot(split[:2 * m, :], ghi[:, cols], preferred_element_type=jnp.float32)
+        small = both[m:] + jnp.dot(split[:m, :], glo[:, cols], preferred_element_type=jnp.float32)
+        return small + both[:m]
+
+    def settle(total):
+        squares = sq_own[...]
+        for k in range(1, n_co):
+            squares = squares + sq_got[k - 1]
+        total = total * lax.rsqrt(squares[0:1] + epsilon)
+        m = total.shape[0]
+        hi = total.astype(jnp.bfloat16)
+        rest = total - hi.astype(jnp.float32)
+        half = rest.astype(jnp.bfloat16)
+        last = (rest - half.astype(jnp.float32)).astype(jnp.bfloat16)
+        three = jnp.concatenate([hi, half, last], axis=0)
+        moved = jnp.dot(three, place[...], preferred_element_type=jnp.float32)
+        return moved[:m] + (moved[m:2 * m] + moved[2 * m:])
+
+    def finish(u):
+        for k in range(1, n_co):
+            for b in range(blocks):
+                part_copy(k, u, b).wait_recv()
+        lag = (co == diag).astype(jnp.int32) * LEAD2
+        first = 2 * u - lag
+
+        @pl.when(first >= 0)
+        def _():
+            total = part[u, pl.ds(pl.multiple_of(co * owned, owned), owned)]
+            for k in range(1, n_co):
+                total = total + got[k - 1, u]
+            moved = settle(total)
+            for i in range(2):
+                at = pl.multiple_of(i * pieces * rows + first * rows, rows)
+                out_ref[pl.ds(at, per_pass), :] = moved[i * per_pass:(i + 1) * per_pass]
+
+    tail_first = pieces - LEAD2
+
+    def tail_load(i, side):
+        where = (core if side == 0 else 1 - core) * (LEAD2 * rows) + i * rows
+        return load(3, side, tail_first + i, passes % 2, where, load_sem.at[i, side, 0])
+
+    def one_pass(u, c):
+        @pl.when(u > 0)
+        def _():
+            forward(2 * u)
+
+        forward(2 * u + 1)
+
+        @pl.when(u >= LEAD2 // 2)
+        def _():
+            for j in range(2):
+                share_diag(2 * u + j - LEAD2)
+
+        for x in range(3):
+            for j in range(2):
+                pass_load(x, 0, j, u).start()
+
+        @pl.when(u >= LEAD2 // 2)
+        def _():
+            for j in range(2):
+                pass_load(3, 0, j, u).start()
+
+        for x in range(3):
+            for j in range(2):
+                sib_copy(x, 2 * u + j, True).wait_recv()
+                pass_load(x, 1, j, u).start()
+
+        @pl.when(u >= LEAD2 // 2)
+        def _():
+            for j in range(2):
+                sib_copy(3, 2 * u + j - LEAD2, True).wait_recv()
+                pass_load(3, 1, j, u).start()
+            for j in range(2):
+                for side in range(2):
+                    pass_load(3, side, j, u).wait()
+
+        for x in range(3):
+            for j in range(2):
+                for side in range(2):
+                    pass_load(x, side, j, u).wait()
+
+        split_queries(u % 2, count)
+
+        def score_block(b, c):
+            part[u, :, block_cols(b)] = scores(count, b)
+            for k in range(1, n_co):
+                part_copy(k, u, b).start()
+
+            @pl.when((u == passes - 1) & (b < LEAD2))
+            def _():
+                share_diag(tail_first + b)
+                tail_load(b, 0).start()
+
+            @pl.when((u == passes - 1) & (b > 0) & (b <= LEAD2))
+            def _():
+                sib_copy(3, tail_first + b - 1, True).wait_recv()
+                tail_load(b - 1, 1).start()
+
+            return c
+
+        lax.fori_loop(0, blocks, score_block, 0)
+
+        @pl.when(u == 1)
+        def _():
+            for k in range(1, n_co):
+                sq_copy(k).wait_recv()
+
+        @pl.when((u > 0) & (u < passes - 1))
+        def _():
+            finish(u - 1)
+
+        return c
+
+    lax.fori_loop(0, passes, one_pass, 0)
+
+    for i in range(blocks, LEAD2):
+        share_diag(tail_first + i)
+        tail_load(i, 0).start()
+    for i in range(min(blocks, LEAD2) - 1, LEAD2):
+        sib_copy(3, tail_first + i, True).wait_recv()
+        tail_load(i, 1).start()
+    for i in range(LEAD2):
+        tail_load(i, 0).wait()
+        tail_load(i, 1).wait()
+    split_queries(passes % 2, tail_rows)
+
+    def tail_block(b, c):
+        @pl.when(b < blocks)
+        def _():
+            tail_part[:, block_cols(b)] = scores(tail_rows, b)
+
+        ready = b - depth
+
+        @pl.when((co != diag) & (ready >= 0) & (ready < blocks))
+        def _():
+            @pl.when(depth > 0)
+            def _():
+                tail_copy(above, ready).wait_recv()
+                cols = block_cols(ready)
+                tail_part[:, cols] = tail_part[:, cols] + tail_got[above, :, cols]
+
+            tail_copy(above, ready).start()
+
+        return c
+
+    lax.fori_loop(0, blocks + n_co - 2, tail_block, 0)
+    finish(passes - 2)
+    finish(passes - 1)
+
+    @pl.when(co == diag)
+    def _():
+        def gather_side(slot):
+            for b in range(blocks):
+                tail_copy(slot, b).wait_recv()
+            tail_part[...] = tail_part[...] + tail_got[slot]
+
+        @pl.when(co > 0)
+        def _():
+            gather_side(0)
+
+        @pl.when(co < n_co - 1)
+        def _():
+            gather_side(1)
+
+        moved = settle(tail_part[...])
+        for i in range(2):
+            at = i * pieces * rows + tail_first * rows
+            out_ref[at:at + LEAD2 * rows, :] = moved[i * LEAD2 * rows:(i + 1) * LEAD2 * rows]
+
+    @pl.when(co != diag)
+    def _():
+        for b in range(blocks):
+            tail_copy(above, b).wait_send()
+
+    def drain(p, c):
+        for way in range(2):
+            own_copy(way, p, False).wait_send()
+            relay_copy(way, p, False).wait_send()
+        for x in range(4):
+            sib_copy(x, p, False).wait_send()
+        return c
+
+    lax.fori_loop(0, pieces, drain, 0)
+
+    def drain_parts(u, c):
+        for k in range(1, n_co):
+            for b in range(blocks):
+                part_copy(k, u, b).wait_send()
+        return c
+
+    lax.fori_loop(0, passes, drain_parts, 0)
+    for k in range(1, n_co):
+        sq_copy(k).wait_send()
+
+
+def plane_shards(n_ex, n_co, train_grads, queries, module_ids, module_scale, example_ids):
+    examples, width = train_grads.shape
+    pieces = queries.shape[0] // 8
+    count = n_ex * 16
+    owned = 32
+    tail_rows = 2 * LEAD2 * 8
+    f32, bf16 = jnp.float32, jnp.bfloat16
+    dma = pltpu.SemaphoreType.DMA
+    smem = pl.BlockSpec(memory_space=pltpu.SMEM)
+    hbm = pl.BlockSpec(memory_space=pl.ANY)
+    vmem = pl.BlockSpec(memory_space=pltpu.VMEM)
+    scores, _ = pl.pallas_call(
+        functools.partial(plane_kernel, n_ex, n_co),
+        out_shape=(
+            jax.ShapeDtypeStruct((2 * queries.shape[0], examples), f32),
+            jax.ShapeDtypeStruct((pieces, n_ex, 8, width), f32),
+        ),
+        in_specs=[smem, smem, hbm, hbm, vmem],
+        out_specs=(vmem, hbm),
+        scratch_shapes=[
+            pltpu.VMEM((width, examples), bf16),
+            pltpu.VMEM((width, examples), bf16),
+            pltpu.VMEM((2, 128, width), f32),
+            pltpu.VMEM((2 * count, width), bf16),
+            pltpu.VMEM((pieces // 2, count, examples), f32),
+            pltpu.VMEM((n_co - 1, pieces // 2, owned, examples), f32),
+            pltpu.VMEM((tail_rows, examples), f32),
+            pltpu.VMEM((2, tail_rows, examples), f32),
+            pltpu.VMEM((examples, examples), bf16),
+            pltpu.VMEM((8, examples), f32),
+            pltpu.VMEM((n_co - 1, 8, examples), f32),
+            dma((2, pieces)),
+            dma((2, pieces)),
+            dma((2, pieces)),
+            dma((2, pieces)),
+            dma((4, pieces)),
+            dma((4, pieces)),
+            dma((n_co - 1, pieces // 2, examples // 256)),
+            dma((n_co - 1, pieces // 2, examples // 256)),
+            dma((examples // 256,)),
+            dma((2, examples // 256)),
+            dma((n_co - 1,)),
+            dma((n_co - 1,)),
+            dma((4, 2, 2)),
+            dma((2,)),
+        ],
+        compiler_params=pltpu.CompilerParams(
+            collective_id=0, has_side_effects=True, vmem_limit_bytes=67043328
+        ),
+    )(module_ids, module_scale, queries, train_grads, example_ids[None, :])
+    return scores
+
+
 def solution(mesh):
+    n_ex, n_co = mesh.shape["ex"], mesh.shape["co"]
+    body = plane_shards if n_ex == 8 and n_ex == 2 * n_co else shards
     return jax.shard_map(
-        functools.partial(shards, mesh.shape["ex"], mesh.shape["co"]),
+        functools.partial(body, n_ex, n_co),
         mesh=mesh,
         in_specs=(P("ex", "co"), P("ex", "co"), P(), P(), P("ex")),
         out_specs=P("co", "ex"),

time: 181 us -> 171 us (0.945); the launches traced: 178 us -> 170 us
  matrix products: 3.88 us -> 0 us
  Pallas kernels: 171 us -> 168 us
  other arithmetic: 2.35 us -> 0 us
  local copies, waits for them, and re-layouts: 0 us -> 2.31 us
    dot_general x1 -> x0, matrix products: 3.88 us -> none  [shards(): lax.dot_general(normed, place, (((1,), (0,)), ((), ())), precision=lax.Pr...]
    pallas_call x1, Pallas kernels: 171 us -> 168 us  [plane_shards(): pl.pallas_call(functools.partial(plane_kernel, n_ex, n_co), out_shape=(ja...]
    unnamed x0 -> x1, local copies, waits for them, and re-layouts: none -> 2.31 us
where the time goes in v1:
time: 171 us; the launch traced here: 170 us
  Pallas kernels  168 us (98%)
  local copies, waits for them, and re-layouts  2.31 us (1%)
    pallas_call x1, Pallas kernels, plane_shards(): pl.pallas_call(functools.partial(plane_kernel, n_ex, n_co), out_shape=(ja...  168 us

profile of v1, /device:TPU:6, one launch (start us, length us, event | category | flops | bytes accessed | tf_op | source)
XLA Modules:
  0.0 170.0 jit_solution(2886194488213501263)
XLA Ops:
  0.0 167.7 %shard_map.55 = (f32[256,1024]{1,0:T(8,128)}, f32[16,8,8,8192]{3,2,1,0:T(8,128)}) custom-call(s32[8]{0:T(128)} %ids_ref.1, f32[224]{0:T(256)} %table_ref.1, f32[128,8192]{1,0:T(8,128)} %q_ref.1, f32[1024,8192]{1,0:T(8,128)} %g_ref.1, s32[1,1024]{1,0:T(1,128)} %bitcast.1), custom_call_target="tpu_custom_call" | custom-call | tf_op jit(solution)/shard_map/pallas_call | solution.py:784
  167.7 2.3 %copy.7 = f32[256,1024]{1,0:T(8,128)} copy(f32[256,1024]{1,0:T(8,128)} %get-tuple-element.6) | data formatting | bytes 2097152

commit v2 on v1

--- a/solution.py
+++ b/solution.py
@@ -357,11 +357,12 @@
     )
 
 
-LEAD2 = 4
-
-
-def plane_kernel(n_ex, n_co, ids_ref, table_ref, q_ref, g_ref, cols_ref, out_ref, buf,
-                 ghi, glo, stage, split, part, got, tail_part, tail_got, place, sq_own, sq_got,
+AHEAD = 2
+UNIT = 16
+
+
+def plane_kernel(n_ex, n_co, ids_any, table_any, q_ref, g_ref, cols_any, out_ref, buf,
+                 ids_ref, table_ref, cols_ref, small_sem, ghi, glo, stage, split, part, got, tail_part, tail_got, place, sq_own, sq_got,
                  own_send, own_recv, rel_send, rel_recv, sib_send, sib_recv,
                  part_send, part_recv, tail_send, tail_recv, sq_send, sq_recv, load_sem, g_sem):
     ex = lax.axis_index("ex")
@@ -370,16 +371,16 @@
     chip = ex // 2
     cx = chip % 2
     cy = chip // 2
-    rows = 8
+    rows = UNIT
     pieces = q_ref.shape[0] // rows
     width = q_ref.shape[1]
     mid = width // 2
     examples = g_ref.shape[0]
-    per_pass = 2 * rows
-    count = n_ex * per_pass
-    owned = 2 * per_pass
-    passes = pieces // 2
-    tail_rows = 2 * LEAD2 * rows
+    count = n_ex * rows
+    owned = 2 * rows
+    early = 4 * rows
+    tail_rows = 2 * AHEAD * rows
+    tail_first = pieces - AHEAD
 
     def chip_at(x):
         fx = cx if x % 2 == 0 else 1 - cx
@@ -392,6 +393,12 @@
 
     def origin(x, side):
         return chip_at(x) * 2 + (core if side == 0 else 1 - core)
+
+    def band(owner):
+        fx = (cx + owner % 2) % 2
+        fy = (cy + owner // 2) % 2
+        place_of = 2 * fx + 3 * fy - 4 * fx * fy
+        return pl.ds(pl.multiple_of(place_of * owned, owned), owned)
 
     barrier = pltpu.get_barrier_semaphore()
     for other in (near[0], near[1], sibling):
@@ -446,7 +453,7 @@
     def part_copy(k, u, b):
         owner = (co + k) % n_co
         return pltpu.make_async_remote_copy(
-            src_ref=part.at[u, pl.ds(pl.multiple_of(owner * owned, owned), owned), block_cols(b)],
+            src_ref=part.at[u, band(owner), block_cols(b)],
             dst_ref=got.at[k - 1, u, :, block_cols(b)],
             send_sem=part_send.at[k - 1, u, b],
             recv_sem=part_recv.at[k - 1, u, b],
@@ -457,12 +464,17 @@
     above = (co > diag).astype(jnp.int32)
     depth = co + above * (n_co - 1 - 2 * co)
 
-    def tail_copy(slot, b):
-        return pltpu.make_async_remote_copy(
-            src_ref=tail_part.at[:, block_cols(b)],
-            dst_ref=tail_got.at[slot, :, block_cols(b)],
-            send_sem=tail_send.at[b],
-            recv_sem=tail_recv.at[slot, b],
+    def grain(g):
+        return pl.ds(g * rows, rows)
+
+    grains = tail_rows // rows
+
+    def tail_copy(slot, b, g):
+        return pltpu.make_async_remote_copy(
+            src_ref=tail_part.at[grain(g), block_cols(b)],
+            dst_ref=tail_got.at[slot, grain(g), block_cols(b)],
+            send_sem=tail_send.at[b, g],
+            recv_sem=tail_recv.at[slot, b, g],
             device_id={"co": (co + 1 - 2 * slot + n_co) % n_co},
             device_id_type=MESH,
         )
@@ -482,7 +494,7 @@
         own_copy(1, p, False).start()
         sib_copy(0, p, False).start()
 
-    for p in range(LEAD2):
+    for p in range(AHEAD):
         send_own(p)
 
     def forward(p):
@@ -491,9 +503,9 @@
         own_copy(0, p, True).wait_recv()
         relay_copy(1, p, False).start()
 
-        @pl.when(p + LEAD2 < pieces)
-        def _():
-            send_own(p + LEAD2)
+        @pl.when(p + AHEAD < pieces)
+        def _():
+            send_own(p + AHEAD)
 
         sib_copy(1, p, False).start()
         sib_copy(2, p, False).start()
@@ -513,6 +525,14 @@
         )
 
     g_load(0).start()
+    smalls = [
+        pltpu.make_async_copy(src, dst, small_sem.at[i])
+        for i, (src, dst) in enumerate([(ids_any, ids_ref), (table_any, table_ref), (cols_any, cols_ref)])
+    ]
+    for copy in smalls:
+        copy.start()
+    for copy in smalls:
+        copy.wait()
 
     local = cols_ref[...] - ex * examples
     for i in range(examples // 128):
@@ -557,18 +577,23 @@
         src = own_rows(p) if x == 0 and side == 0 else buf.at[p, origin(x, side)]
         return pltpu.make_async_copy(src, stage.at[slot, pl.ds(pl.multiple_of(row, rows), rows)], sem)
 
-    def pass_load(x, side, j, u):
-        p = 2 * u + j - (LEAD2 if x == 3 else 0)
-        return load(x, side, p, u % 2, origin(x, side) * per_pass + j * rows, load_sem.at[x, side, j])
-
-    def split_queries(slot, m):
+    def pass_load(x, side, u):
+        p = u - (AHEAD if x == 3 else 0)
+        at = (0, 2, 3, 1)[x] * owned + (core if side == 0 else 1 - core) * rows
+        return load(x, side, p, u % 2, at, load_sem.at[x, side])
+
+    def tail_load(i, side):
+        at = (core if side == 0 else 1 - core) * (AHEAD * rows) + i * rows
+        return load(3, side, tail_first + i, pieces % 2, at, load_sem.at[i, side])
+
+    def split_queries(slot, first, size, m):
         def body(j, c):
             col = pl.ds(pl.multiple_of(j * strip, strip), strip)
             scale = table_ref[ids_ref[(co * width + j * strip) // PROJ]]
-            x = stage[slot, :m, col] * scale
+            x = stage[slot, first:first + size, col] * scale
             hi = x.astype(jnp.bfloat16)
-            split[pl.ds(0, m), col] = hi
-            split[pl.ds(m, m), col] = (x - hi.astype(jnp.float32)).astype(jnp.bfloat16)
+            split[first:first + size, col] = hi
+            split[m + first:m + first + size, col] = (x - hi.astype(jnp.float32)).astype(jnp.bfloat16)
             return c
 
         lax.fori_loop(0, width // strip, body, 0)
@@ -597,81 +622,92 @@
         for k in range(1, n_co):
             for b in range(blocks):
                 part_copy(k, u, b).wait_recv()
-        lag = (co == diag).astype(jnp.int32) * LEAD2
-        first = 2 * u - lag
+        lag = (co == diag).astype(jnp.int32) * AHEAD
+        first = u - lag
 
         @pl.when(first >= 0)
         def _():
-            total = part[u, pl.ds(pl.multiple_of(co * owned, owned), owned)]
+            total = part[u, band(co)]
             for k in range(1, n_co):
                 total = total + got[k - 1, u]
             moved = settle(total)
             for i in range(2):
                 at = pl.multiple_of(i * pieces * rows + first * rows, rows)
-                out_ref[pl.ds(at, per_pass), :] = moved[i * per_pass:(i + 1) * per_pass]
-
-    tail_first = pieces - LEAD2
-
-    def tail_load(i, side):
-        where = (core if side == 0 else 1 - core) * (LEAD2 * rows) + i * rows
-        return load(3, side, tail_first + i, passes % 2, where, load_sem.at[i, side, 0])
+                out_ref[pl.ds(at, rows), :] = moved[i * rows:(i + 1) * rows]
+
+    def early_own(u):
+        pass_load(0, 0, u).start()
+
+        @pl.when(u >= AHEAD)
+        def _():
+            share_diag(u - AHEAD)
+            pass_load(3, 0, u).start()
+
+    def early_sibling(u):
+        sib_copy(0, u, True).wait_recv()
+        pass_load(0, 1, u).start()
+
+        @pl.when(u >= AHEAD)
+        def _():
+            sib_copy(3, u - AHEAD, True).wait_recv()
+            pass_load(3, 1, u).start()
+
+    early_own(0)
+    early_sibling(0)
 
     def one_pass(u, c):
-        @pl.when(u > 0)
-        def _():
-            forward(2 * u)
-
-        forward(2 * u + 1)
-
-        @pl.when(u >= LEAD2 // 2)
-        def _():
-            for j in range(2):
-                share_diag(2 * u + j - LEAD2)
-
-        for x in range(3):
-            for j in range(2):
-                pass_load(x, 0, j, u).start()
-
-        @pl.when(u >= LEAD2 // 2)
-        def _():
-            for j in range(2):
-                pass_load(3, 0, j, u).start()
-
-        for x in range(3):
-            for j in range(2):
-                sib_copy(x, 2 * u + j, True).wait_recv()
-                pass_load(x, 1, j, u).start()
-
-        @pl.when(u >= LEAD2 // 2)
-        def _():
-            for j in range(2):
-                sib_copy(3, 2 * u + j - LEAD2, True).wait_recv()
-                pass_load(3, 1, j, u).start()
-            for j in range(2):
-                for side in range(2):
-                    pass_load(3, side, j, u).wait()
-
-        for x in range(3):
-            for j in range(2):
-                for side in range(2):
-                    pass_load(x, side, j, u).wait()
-
-        split_queries(u % 2, count)
+        for side in range(2):
+            pass_load(0, side, u).wait()
+
+        @pl.when(u >= AHEAD)
+        def _():
+            for side in range(2):
+                pass_load(3, side, u).wait()
+
+        split_queries(u % 2, 0, early, count)
+
+        @pl.when(u > 1)
+        def _():
+            forward(u)
+
+        for x in (1, 2):
+            pass_load(x, 0, u).start()
+        for x in (1, 2):
+            sib_copy(x, u, True).wait_recv()
+            pass_load(x, 1, u).start()
+        for x in (1, 2):
+            for side in range(2):
+                pass_load(x, side, u).wait()
+        split_queries(u % 2, early, count - early, count)
 
         def score_block(b, c):
             part[u, :, block_cols(b)] = scores(count, b)
             for k in range(1, n_co):
                 part_copy(k, u, b).start()
 
-            @pl.when((u == passes - 1) & (b < LEAD2))
+            @pl.when((u == 0) & (b == 0))
             def _():
-                share_diag(tail_first + b)
-                tail_load(b, 0).start()
-
-            @pl.when((u == passes - 1) & (b > 0) & (b <= LEAD2))
+                forward(1)
+
+            @pl.when((u < pieces - 1) & (b == 1))
             def _():
-                sib_copy(3, tail_first + b - 1, True).wait_recv()
-                tail_load(b - 1, 1).start()
+                early_own(u + 1)
+
+            @pl.when((u < pieces - 1) & (b == 2))
+            def _():
+                early_sibling(u + 1)
+
+            @pl.when((u == pieces - 1) & (b == 1))
+            def _():
+                share_diag(tail_first)
+                tail_load(0, 0).start()
+
+            @pl.when((u == pieces - 1) & (b == 2))
+            def _():
+                sib_copy(3, tail_first, True).wait_recv()
+                tail_load(0, 1).start()
+                share_diag(tail_first + 1)
+                tail_load(1, 0).start()
 
             return c
 
@@ -682,24 +718,20 @@
             for k in range(1, n_co):
                 sq_copy(k).wait_recv()
 
-        @pl.when((u > 0) & (u < passes - 1))
+        @pl.when((u > 0) & (u < pieces - 1))
         def _():
             finish(u - 1)
 
         return c
 
-    lax.fori_loop(0, passes, one_pass, 0)
-
-    for i in range(blocks, LEAD2):
-        share_diag(tail_first + i)
-        tail_load(i, 0).start()
-    for i in range(min(blocks, LEAD2) - 1, LEAD2):
-        sib_copy(3, tail_first + i, True).wait_recv()
-        tail_load(i, 1).start()
-    for i in range(LEAD2):
+    lax.fori_loop(0, pieces, one_pass, 0)
+
+    sib_copy(3, tail_first + 1, True).wait_recv()
+    tail_load(1, 1).start()
+    for i in range(AHEAD):
         tail_load(i, 0).wait()
         tail_load(i, 1).wait()
-    split_queries(passes % 2, tail_rows)
+    split_queries(pieces % 2, 0, tail_rows, tail_rows)
 
     def tail_block(b, c):
         @pl.when(b < blocks)
@@ -710,25 +742,27 @@
 
         @pl.when((co != diag) & (ready >= 0) & (ready < blocks))
         def _():
-            @pl.when(depth > 0)
-            def _():
-                tail_copy(above, ready).wait_recv()
-                cols = block_cols(ready)
-                tail_part[:, cols] = tail_part[:, cols] + tail_got[above, :, cols]
-
-            tail_copy(above, ready).start()
+            cols = block_cols(ready)
+            for g in range(grains):
+                @pl.when(depth > 0)
+                def _():
+                    tail_copy(above, ready, g).wait_recv()
+                    tail_part[grain(g), cols] = tail_part[grain(g), cols] + tail_got[above, grain(g), cols]
+
+                tail_copy(above, ready, g).start()
 
         return c
 
     lax.fori_loop(0, blocks + n_co - 2, tail_block, 0)
-    finish(passes - 2)
-    finish(passes - 1)
+    finish(pieces - 2)
+    finish(pieces - 1)
 
     @pl.when(co == diag)
     def _():
         def gather_side(slot):
             for b in range(blocks):
-                tail_copy(slot, b).wait_recv()
+                for g in range(grains):
+                    tail_copy(slot, b, g).wait_recv()
             tail_part[...] = tail_part[...] + tail_got[slot]
 
         @pl.when(co > 0)
@@ -742,12 +776,13 @@
         moved = settle(tail_part[...])
         for i in range(2):
             at = i * pieces * rows + tail_first * rows
-            out_ref[at:at + LEAD2 * rows, :] = moved[i * LEAD2 * rows:(i + 1) * LEAD2 * rows]
+            out_ref[at:at + AHEAD * rows, :] = moved[i * AHEAD * rows:(i + 1) * AHEAD * rows]
 
     @pl.when(co != diag)
     def _():
         for b in range(blocks):
-            tail_copy(above, b).wait_send()
+            for g in range(grains):
+                tail_copy(above, b, g).wait_send()
 
     def drain(p, c):
         for way in range(2):
@@ -765,37 +800,40 @@
                 part_copy(k, u, b).wait_send()
         return c
 
-    lax.fori_loop(0, passes, drain_parts, 0)
+    lax.fori_loop(0, pieces, drain_parts, 0)
     for k in range(1, n_co):
         sq_copy(k).wait_send()
 
 
 def plane_shards(n_ex, n_co, train_grads, queries, module_ids, module_scale, example_ids):
     examples, width = train_grads.shape
-    pieces = queries.shape[0] // 8
-    count = n_ex * 16
-    owned = 32
-    tail_rows = 2 * LEAD2 * 8
+    pieces = queries.shape[0] // UNIT
+    count = n_ex * UNIT
+    owned = 2 * UNIT
+    tail_rows = 2 * AHEAD * UNIT
     f32, bf16 = jnp.float32, jnp.bfloat16
     dma = pltpu.SemaphoreType.DMA
-    smem = pl.BlockSpec(memory_space=pltpu.SMEM)
     hbm = pl.BlockSpec(memory_space=pl.ANY)
     vmem = pl.BlockSpec(memory_space=pltpu.VMEM)
     scores, _ = pl.pallas_call(
         functools.partial(plane_kernel, n_ex, n_co),
         out_shape=(
             jax.ShapeDtypeStruct((2 * queries.shape[0], examples), f32),
-            jax.ShapeDtypeStruct((pieces, n_ex, 8, width), f32),
+            jax.ShapeDtypeStruct((pieces, n_ex, UNIT, width), f32),
         ),
-        in_specs=[smem, smem, hbm, hbm, vmem],
+        in_specs=[hbm, hbm, hbm, hbm, hbm],
         out_specs=(vmem, hbm),
         scratch_shapes=[
+            pltpu.SMEM(module_ids.shape, jnp.int32),
+            pltpu.SMEM(module_scale.shape, f32),
+            pltpu.VMEM((1, examples), jnp.int32),
+            dma((3,)),
             pltpu.VMEM((width, examples), bf16),
             pltpu.VMEM((width, examples), bf16),
             pltpu.VMEM((2, 128, width), f32),
             pltpu.VMEM((2 * count, width), bf16),
-            pltpu.VMEM((pieces // 2, count, examples), f32),
-            pltpu.VMEM((n_co - 1, pieces // 2, owned, examples), f32),
+            pltpu.VMEM((pieces, count, examples), f32),
+            pltpu.VMEM((n_co - 1, pieces, owned, examples), f32),
             pltpu.VMEM((tail_rows, examples), f32),
             pltpu.VMEM((2, tail_rows, examples), f32),
             pltpu.VMEM((examples, examples), bf16),
@@ -807,13 +845,13 @@
             dma((2, pieces)),
             dma((4, pieces)),
             dma((4, pieces)),
-            dma((n_co - 1, pieces // 2, examples // 256)),
-            dma((n_co - 1, pieces // 2, examples // 256)),
-            dma((examples // 256,)),
-            dma((2, examples // 256)),
+            dma((n_co - 1, pieces, examples // 256)),
+            dma((n_co - 1, pieces, examples // 256)),
+            dma((examples // 256, 2 * AHEAD)),
+            dma((2, examples // 256, 2 * AHEAD)),
             dma((n_co - 1,)),
             dma((n_co - 1,)),
-            dma((4, 2, 2)),
+            dma((4, 2)),
             dma((2,)),
         ],
         compiler_params=pltpu.CompilerParams(

time: 171 us -> 167 us (0.977)
  Pallas kernels: 168 us -> 164 us
    pallas_call x1, Pallas kernels: 168 us -> 164 us  [plane_shards(): pl.pallas_call(functools.partial(plane_kernel, n_ex, n_co), out_shape=(ja...]
where the time goes in v2:
time: 167 us; the launch traced here: 166 us
  Pallas kernels  164 us (98%)
  local copies, waits for them, and re-layouts  2.31 us (1%)
    pallas_call x1, Pallas kernels, plane_shards(): pl.pallas_call(functools.partial(plane_kernel, n_ex, n_co), out_shape=(ja...  164 us

profile of v2, /device:TPU:6, one launch (start us, length us, event | category | flops | bytes accessed | tf_op | source)
XLA Modules:
  0.0 166.2 jit_solution(5647252266276407957)
XLA Ops:
  0.0 163.9 %shard_map.55 = (f32[256,1024]{1,0:T(8,128)}, f32[8,8,16,8192]{3,2,1,0:T(8,128)}) custom-call(s32[8]{0:T(128)} %ids_any.1, f32[224]{0:T(256)} %table_any.1, f32[128,8192]{1,0:T(8,128)} %q_ref.1, f32[1024,8192]{1,0:T(8,128)} %g_ref.1, s32[1,1024]{1,0:T(1,128)} %bitcast.1), custom_call_target="tpu_custom_call" | custom-call | tf_op jit(solution)/shard_map/pallas_call | solution.py:818
  163.9 2.3 %copy.7 = f32[256,1024]{1,0:T(8,128)} copy(f32[256,1024]{1,0:T(8,128)} %get-tuple-element.6) | data formatting | bytes 2097152

commit v3 on v2

--- a/solution.py
+++ b/solution.py
@@ -361,8 +361,8 @@
 UNIT = 16
 
 
-def plane_kernel(n_ex, n_co, ids_any, table_any, q_ref, g_ref, cols_any, out_ref, buf,
-                 ids_ref, table_ref, cols_ref, small_sem, ghi, glo, stage, split, part, got, tail_part, tail_got, place, sq_own, sq_got,
+def plane_kernel(n_ex, n_co, ids_any, table_any, q_ref, g_ref, cols_any, final_ref, buf,
+                 ids_ref, table_ref, cols_ref, small_sem, out_ref, out_sem, ghi, glo, stage, split, tail_split, part, got, tail_part, tail_got, place, sq_own, sq_got,
                  own_send, own_recv, rel_send, rel_recv, sib_send, sib_recv,
                  part_send, part_recv, tail_send, tail_recv, sq_send, sq_recv, load_sem, g_sem):
     ex = lax.axis_index("ex")
@@ -502,13 +502,12 @@
         relay_copy(0, p, False).start()
         own_copy(0, p, True).wait_recv()
         relay_copy(1, p, False).start()
+        sib_copy(2, p, False).start()
+        sib_copy(1, p, False).start()
 
         @pl.when(p + AHEAD < pieces)
         def _():
             send_own(p + AHEAD)
-
-        sib_copy(1, p, False).start()
-        sib_copy(2, p, False).start()
 
     def share_diag(p):
         relay_copy(0, p, True).wait_recv()
@@ -583,25 +582,25 @@
         return load(x, side, p, u % 2, at, load_sem.at[x, side])
 
     def tail_load(i, side):
-        at = (core if side == 0 else 1 - core) * (AHEAD * rows) + i * rows
+        at = i * owned + (core if side == 0 else 1 - core) * rows
         return load(3, side, tail_first + i, pieces % 2, at, load_sem.at[i, side])
 
-    def split_queries(slot, first, size, m):
+    def split_queries(halves, slot, first, size, m):
         def body(j, c):
             col = pl.ds(pl.multiple_of(j * strip, strip), strip)
             scale = table_ref[ids_ref[(co * width + j * strip) // PROJ]]
             x = stage[slot, first:first + size, col] * scale
             hi = x.astype(jnp.bfloat16)
-            split[first:first + size, col] = hi
-            split[m + first:m + first + size, col] = (x - hi.astype(jnp.float32)).astype(jnp.bfloat16)
+            halves[first:first + size, col] = hi
+            halves[m + first:m + first + size, col] = (x - hi.astype(jnp.float32)).astype(jnp.bfloat16)
             return c
 
         lax.fori_loop(0, width // strip, body, 0)
 
-    def scores(m, b):
+    def scores(halves, m, b):
         cols = block_cols(b)
-        both = jnp.dot(split[:2 * m, :], ghi[:, cols], preferred_element_type=jnp.float32)
-        small = both[m:] + jnp.dot(split[:m, :], glo[:, cols], preferred_element_type=jnp.float32)
+        both = jnp.dot(halves[:2 * m, :], ghi[:, cols], preferred_element_type=jnp.float32)
+        small = both[m:] + jnp.dot(halves[:m, :], glo[:, cols], preferred_element_type=jnp.float32)
         return small + both[:m]
 
     def settle(total):
@@ -618,6 +617,10 @@
         moved = jnp.dot(three, place[...], preferred_element_type=jnp.float32)
         return moved[:m] + (moved[m:2 * m] + moved[2 * m:])
 
+    def out_copy(i, p):
+        at = pl.ds(pl.multiple_of(i * pieces * rows + p * rows, rows), rows)
+        return pltpu.make_async_copy(out_ref.at[at], final_ref.at[at], out_sem.at[i, p])
+
     def finish(u):
         for k in range(1, n_co):
             for b in range(blocks):
@@ -634,6 +637,7 @@
             for i in range(2):
                 at = pl.multiple_of(i * pieces * rows + first * rows, rows)
                 out_ref[pl.ds(at, rows), :] = moved[i * rows:(i + 1) * rows]
+                out_copy(i, first).start()
 
     def early_own(u):
         pass_load(0, 0, u).start()
@@ -664,24 +668,24 @@
             for side in range(2):
                 pass_load(3, side, u).wait()
 
-        split_queries(u % 2, 0, early, count)
+        split_queries(split, u % 2, 0, early, count)
 
         @pl.when(u > 1)
         def _():
             forward(u)
 
-        for x in (1, 2):
+        for x in (2, 1):
             pass_load(x, 0, u).start()
-        for x in (1, 2):
+        for x in (2, 1):
             sib_copy(x, u, True).wait_recv()
             pass_load(x, 1, u).start()
-        for x in (1, 2):
+        for x in (2, 1):
             for side in range(2):
                 pass_load(x, side, u).wait()
-        split_queries(u % 2, early, count - early, count)
+            split_queries(split, u % 2, early + (x - 1) * owned, owned, count)
 
         def score_block(b, c):
-            part[u, :, block_cols(b)] = scores(count, b)
+            part[u, :, block_cols(b)] = scores(split, count, b)
             for k in range(1, n_co):
                 part_copy(k, u, b).start()
 
@@ -731,12 +735,12 @@
     for i in range(AHEAD):
         tail_load(i, 0).wait()
         tail_load(i, 1).wait()
-    split_queries(pieces % 2, 0, tail_rows, tail_rows)
+        split_queries(tail_split, pieces % 2, i * owned, owned, tail_rows)
 
     def tail_block(b, c):
         @pl.when(b < blocks)
         def _():
-            tail_part[:, block_cols(b)] = scores(tail_rows, b)
+            tail_part[:, block_cols(b)] = scores(tail_split, tail_rows, b)
 
         ready = b - depth
 
@@ -774,9 +778,12 @@
             gather_side(1)
 
         moved = settle(tail_part[...])
-        for i in range(2):
-            at = i * pieces * rows + tail_first * rows
-            out_ref[at:at + AHEAD * rows, :] = moved[i * AHEAD * rows:(i + 1) * AHEAD * rows]
+        for i in range(AHEAD):
+            for j in range(2):
+                at = j * pieces * rows + (tail_first + i) * rows
+                row = i * owned + j * rows
+                out_ref[at:at + rows, :] = moved[row:row + rows]
+                out_copy(j, tail_first + i).start()
 
     @pl.when(co != diag)
     def _():
@@ -801,8 +808,34 @@
         return c
 
     lax.fori_loop(0, pieces, drain_parts, 0)
+
+    def drain_out(p, c):
+        for i in range(2):
+            out_copy(i, p).wait()
+        return c
+
+    lax.fori_loop(0, pieces, drain_out, 0)
     for k in range(1, n_co):
         sq_copy(k).wait_send()
+
+
+MOVES = 4
+
+
+def move_out(src, dst, box, in_sem, out_sem):
+    size = src.shape[0] // MOVES
+
+    def copy(a, b, sem, j):
+        at = pl.ds(j * size, size)
+        return pltpu.make_async_copy(a.at[at], b.at[at], sem.at[j])
+
+    for j in range(MOVES):
+        copy(src, box, in_sem, j).start()
+    for j in range(MOVES):
+        copy(src, box, in_sem, j).wait()
+        copy(box, dst, out_sem, j).start()
+    for j in range(MOVES):
+        copy(box, dst, out_sem, j).wait()
 
 
 def plane_shards(n_ex, n_co, train_grads, queries, module_ids, module_scale, example_ids):
@@ -814,7 +847,6 @@
     f32, bf16 = jnp.float32, jnp.bfloat16
     dma = pltpu.SemaphoreType.DMA
     hbm = pl.BlockSpec(memory_space=pl.ANY)
-    vmem = pl.BlockSpec(memory_space=pltpu.VMEM)
     scores, _ = pl.pallas_call(
         functools.partial(plane_kernel, n_ex, n_co),
         out_shape=(
@@ -822,16 +854,19 @@
             jax.ShapeDtypeStruct((pieces, n_ex, UNIT, width), f32),
         ),
         in_specs=[hbm, hbm, hbm, hbm, hbm],
-        out_specs=(vmem, hbm),
+        out_specs=(hbm, hbm),
         scratch_shapes=[
             pltpu.SMEM(module_ids.shape, jnp.int32),
             pltpu.SMEM(module_scale.shape, f32),
             pltpu.VMEM((1, examples), jnp.int32),
             dma((3,)),
+            pltpu.VMEM((2 * queries.shape[0], examples), f32),
+            dma((2, pieces)),
             pltpu.VMEM((width, examples), bf16),
             pltpu.VMEM((width, examples), bf16),
             pltpu.VMEM((2, 128, width), f32),
             pltpu.VMEM((2 * count, width), bf16),
+            pltpu.VMEM((2 * tail_rows, width), bf16),
             pltpu.VMEM((pieces, count, examples), f32),
             pltpu.VMEM((n_co - 1, pieces, owned, examples), f32),
             pltpu.VMEM((tail_rows, examples), f32),
@@ -858,7 +893,13 @@
             collective_id=0, has_side_effects=True, vmem_limit_bytes=67043328
         ),
     )(module_ids, module_scale, queries, train_grads, example_ids[None, :])
-    return scores
+    return pl.pallas_call(
+        move_out,
+        out_shape=jax.ShapeDtypeStruct(scores.shape, f32),
+        in_specs=[hbm],
+        out_specs=hbm,
+        scratch_shapes=[pltpu.VMEM(scores.shape, f32), dma((MOVES,)), dma((MOVES,))],
+    )(scores)
 
 
 def solution(mesh):

time: 167 us -> 166 us (level)
  local copies, waits for them, and re-layouts: 2.31 us -> 0 us
    unnamed x1 -> x0, local copies, waits for them, and re-layouts: 2.31 us -> none
    pallas_call x0 -> x1, Pallas kernels: none -> 1.98 us  [plane_shards(): pl.pallas_call(move_out, out_shape=jax.ShapeDtypeStruct(scores.shape, f32...]
where the time goes in v3:
time: 166 us; the launch traced here: 165 us
  Pallas kernels  165 us (99%)
    pallas_call x1, Pallas kernels, plane_shards(): pl.pallas_call(functools.partial(plane_kernel, n_ex, n_co), out_shape=(ja...  163 us

profile of v3, /device:TPU:6, one launch (start us, length us, event | category | flops | bytes accessed | tf_op | source)
XLA Modules:
  0.0 165.1 jit_solution(17767457291053828632)
XLA Ops:
  0.0 163.1 %shard_map.55 = (f32[256,1024]{1,0:T(8,128)}, f32[8,8,16,8192]{3,2,1,0:T(8,128)}) custom-call(s32[8]{0:T(128)} %ids_any.1, f32[224]{0:T(256)} %table_any.1, f32[128,8192]{1,0:T(8,128)} %q_ref.1, f32[1024,8192]{1,0:T(8,128)} %g_ref.1, s32[1,1024]{1,0:T(1,128)} %bitcast.1), custom_call_target="tpu_custom_call" | custom-call | tf_op jit(solution)/shard_map/pallas_call | solution.py:850
  163.1 2.0 %shard_map.56 = f32[256,1024]{1,0:T(8,128)} custom-call(f32[256,1024]{1,0:T(8,128)} %get-tuple-element.6.src), custom_call_target="tpu_custom_call" | custom-call | tf_op jit(solution)/shard_map/pallas_call | solution.py:896
